TPU v7x, 128 devices: a whole 4x4x4 slice. The times are simulated.
128 devices in a mesh: ctx: 32 (over z, x, core), tp: 4 (over y).
Axes of the slice: x: 4, y: 4, z: 4, core: 2. Of those that a mesh axis runs over, the one named last changes fastest.
Arguments:
- tokens: bfloat16 [4096, 4096], P('ctx', 'tp'), may hold values from -6 to 6
- in_weight: bfloat16 [4096, 3, 4096], P('ctx', None, 'tp'), may hold values from -0.09375 to 0.09375
- conv_taps: float32 [3, 3, 4096], P(None, None, 'tp'), may hold values from -2.5 to 2.5
- decay_rate: float32 [16, 4096], P(None, 'tp'), may hold values from 0 to 0.034, as said below
- residue: float32 [16, 4096], P(None, 'tp'), may hold values from -1 to 1
- skip: float32 [4096], P('tp'), may hold values from -1 to 1
Outputs:
- mixed: bfloat16 [4096, 4096], P('ctx', 'tp')
Inputs may be any that keep to these rules, and one draw needn't show every extreme that they name: `decay_rate`: positive decay rates of the poles.
All inputs are finite; a program needn't handle non-finite values.
Results may differ from a plain program's by a relative error of at most 0.0063.
Values may be sent and summed in bfloat16 or wider, within the bound.
A program may use at most 128 MiB of HBM per device.

v0:
```python
import math
import jax
import jax.numpy as jnp
from jax import lax
from jax.sharding import PartitionSpec as P


def passed_along(array, axis, by):
    peers = lax.axis_size(axis)
    pairs = [(i, i + by) for i in range(peers) if 0 <= i + by < peers]
    return lax.ppermute(array, axis, pairs)


def entering(array, axis, combine, identity):
    peers, here = (lax.axis_size(axis), lax.axis_index(axis))
    everything = jax.tree.map(lambda part: lax.all_gather(part, axis), array)
    start = jax.tree.map(
        lambda part, zero: jnp.broadcast_to(jnp.asarray(zero, part.dtype), part.shape),
        array,
        identity,
    )

    def turn(k, before):
        reached = k < here
        new = combine(before, jax.tree.map(lambda part: part[k], everything))
        return jax.tree.map(lambda a, b: jnp.where(reached, a, b), new, before)

    return lax.fori_loop(0, peers, turn, start)


def link(earlier, later):
    return (earlier[0] * later[0], later[0] * earlier[1] + later[1])


def per_device(tokens, in_weight, conv_taps, decay_rate, residue, skip):
    rows = tokens.shape[0]
    chans = in_weight.shape[2]
    whole = lax.all_gather(tokens, "tp", axis=1, tiled=True)
    piece = lax.all_gather(in_weight, "ctx", axis=0, tiled=True)
    sums = tuple(
        (jnp.dot(whole, piece[:, g, :], preferred_element_type=jnp.float32) for g in range(3))
    )
    projected = jnp.stack([total.astype(jnp.bfloat16) for total in sums], axis=0)
    edge_out = passed_along(projected[:, rows - 2 :, :], "ctx", 1)
    extended = jnp.concatenate([edge_out, projected], axis=1)
    values = lax.optimization_barrier(extended).astype(jnp.float32)
    filtered = (
        conv_taps[0][:, None, :] * values[:, 2:, :]
        + conv_taps[1][:, None, :] * values[:, 1:-1, :]
        + conv_taps[2][:, None, :] * values[:, :-2, :]
    )
    query = filtered[0]
    gated = filtered[1] * filtered[2]
    span = math.gcd(rows, 32)
    blocks = rows // span
    offsets = jnp.arange(span, dtype=jnp.float32)
    powers = jnp.exp(-decay_rate[None] * offsets[:, None, None])
    response = jnp.sum(residue[None] * powers, axis=1)
    lags = jnp.arange(span)[:, None] - jnp.arange(span)[None, :]
    toeplitz = jnp.where((lags >= 0)[:, :, None], response[jnp.clip(lags, 0, span - 1)], 0.0)
    blocked = gated.reshape(blocks, span, chans)
    inside = jnp.einsum("tsc,bsc->btc", toeplitz, blocked, precision=lax.Precision.HIGHEST)
    tails = jnp.exp(-decay_rate[None] * (span - 1.0 - offsets)[:, None, None])
    ends = jnp.einsum("spc,bsc->bpc", tails, blocked, precision=lax.Precision.HIGHEST)
    block_decay = jnp.broadcast_to(jnp.exp(-decay_rate * span)[None], ends.shape)
    after = lax.associative_scan(link, (block_decay, ends), axis=0)[1]
    final = after[blocks - 1]
    starts = jnp.concatenate([jnp.zeros_like(after[:1]), after[: blocks - 1]], axis=0)
    segment = jnp.exp(-decay_rate * rows)
    carried = entering(
        (segment, final), "ctx", link, (jnp.ones_like(final), jnp.zeros_like(final))
    )[1]
    block_starts = (span * jnp.arange(blocks, dtype=jnp.float32))[:, None, None]
    begin = starts + jnp.exp(-decay_rate[None] * block_starts) * carried[None]
    leading = residue[None] * jnp.exp(-decay_rate[None] * (offsets + 1.0)[:, None, None])
    convolved = inside + jnp.einsum("tpc,bpc->btc", leading, begin, precision=lax.Precision.HIGHEST)
    convolved = convolved.reshape(rows, chans)
    return (query * (convolved + skip[None, :] * gated)).astype(jnp.bfloat16)


def solution(mesh):
    placed = (
        P("ctx", "tp"),
        P("ctx", None, "tp"),
        P(None, None, "tp"),
        P(None, "tp"),
        P(None, "tp"),
        P("tp"),
    )
    return jax.shard_map(
        per_device, mesh=mesh, in_specs=placed, out_specs=P("ctx", "tp"), check_vma=False
    )
```

profile of v0, /device:TPU:32, one launch (start us, length us, event | category | flops | bytes accessed | tf_op | source)
XLA Modules:
  0.0 293.2 jit_solution(15202066247814389937)
XLA Ops:
  8.1 1.5 multiply_exponential_fusion
  10.4 24.7 %all-gather.6.cloned.1.call-done = bf16[128,4096]{1,0:T(8,128)(2,1)} async-done(((bf16[128,1024]{1,0:T(8,128)(2,1)}), bf16[128,4096]{1,0:T(8,128)(2,1)}) %all-gather.6.cloned.1.call-update) | async-done | bytes 1048592 | tf_op jit(solution)/shard_map/all_gather | solution.py:38
  35.1 94.1 %all-gather.8.cloned.1.call-done = bf16[4096,3,1024]{2,0,1:T(8,128)(2,1)} async-done(((bf16[128,3,1024]{2,0,1:T(8,128)(2,1)}), bf16[4096,3,1024]{2,0,1:T(8,128)(2,1)}) %all-gather.8.cloned.1.call-update) | async-done | bytes 25165840 | tf_op jit(solution)/shard_map/all_gather | solution.py:39
  129.2 5.0 %fusion.27 = bf16[1,128,1024]{2,1,0:T(8,128)(2,1)S(1)} fusion(bf16[128,4096]{1,0:T(8,128)(2,1)} %all-gather.6.cloned.1.call-done, bf16[4096,3,1024]{2,0,1:T(8,128)(2,1)} %all-gather.8.cloned.1.call-done), kind=kOutput, calls=%fused_computation.36 | convolution fusion | flops 1073872896 | bytes 9699328 | tf_op jit(solution)/shard_map/dot_general | solution.py:41
  134.1 4.6 %fusion.28 = bf16[1,128,1024]{2,1,0:T(8,128)(2,1)S(1)} fusion(bf16[128,4096]{1,0:T(8,128)(2,1)S(1)} %copy-done.15, bf16[4096,3,1024]{2,0,1:T(8,128)(2,1)} %all-gather.8.cloned.1.call-done), kind=kOutput, calls=%fused_computation.37 | convolution fusion | flops 1073872896 | bytes 9699328 | tf_op jit(solution)/shard_map/dot_general | solution.py:41
  138.8 4.7 %fusion.29 = bf16[1,128,1024]{2,1,0:T(8,128)(2,1)S(1)} fusion(bf16[128,4096]{1,0:T(8,128)(2,1)S(1)} %copy-done.15, bf16[4096,3,1024]{2,0,1:T(8,128)(2,1)} %all-gather.8.cloned.1.call-done), kind=kOutput, calls=%fused_computation.38 | convolution fusion | flops 1073872896 | bytes 9699328 | tf_op jit(solution)/shard_map/dot_general | solution.py:41
  143.5 2.4 collective-permute-start
  146.1 4.6 %collective-permute-done = bf16[3,2,1024]{2,1,0:T(2,128)(2,1)S(1)} collective-permute-done((bf16[3,2,1024]{2,1,0:T(2,128)(2,1)S(1)}, bf16[3,2,1024]{2,1,0:T(2,128)(2,1)S(1)}, u32[]{:S(2)}, u32[]{:S(2)}) %collective-permute-start) | collective-permute-done | bytes 12320 | tf_op jit(solution)/shard_map/ppermute | solution.py:11
  151.6 1.1 copy-done
  153.5 14.8 %fusion.10 = f32[1024,4,16]{2,1,0:T(4,128)} fusion(f32[4,32,1024]{1,0,2:T(4,128)S(1)} %copy.65, f32[32]{0:T(128)S(1)} %iota_subtract_fusion, f32[16,1024]{0,1:T(8,128)S(1)} %copy.62), kind=kOutput, calls=%fused_computation.16 | convolution fusion | flops 25690112 | bytes 852096 | tf_op jit(solution)/shard_map/spc,bsc->bpc/dot_general | solution.py:64
  168.4 1.9 copy.67
  171.1 1.0 copy.61
  172.2 15.3 %multiply_reduce_fusion = f32[32,1024]{0,1:T(8,128)S(1)} fusion(f32[16,1024]{0,1:T(8,128)S(1)} %copy.62, f32[16,1024]{0,1:T(8,128)} %copy.61), kind=kLoop, calls=%fused_computation.20 | loop fusion | flops 1540096 | bytes 262144 | tf_op jit(solution)/shard_map/reduce_sum | solution.py:58
  187.7 5.4 %gather_fusion = f32[1024,1024]{1,0:T(8,128)} fusion(f32[32,1024]{1,0:T(8,128)S(1)} %copy.63, s32[1024]{0:T(1024)S(1)} %broadcast_clamp_fusion), kind=kCustom, calls=%fused_computation | custom fusion | bytes 8392704 | tf_op jit(solution)/shard_map/gather | solution.py:60
  193.2 14.4 %copy.64 = f32[32,32,1024]{1,0,2:T(8,128)} copy(f32[32,32,1024]{2,1,0:T(8,128)} %bitcast.79) | data formatting | bytes 8388608 | tf_op jit(solution)/shard_map/gather | solution.py:60
  208.4 29.5 %fusion.1 = f32[1024,4,32]{2,1,0:T(4,128)} fusion(f32[4,32,1024]{1,0,2:T(4,128)S(1)} %copy.65, f32[32,32,1024]{1,0,2:T(8,128)} %copy.64, pred[32,32]{1,0:T(8,128)(4,1)S(1)} %subtract_compare_fusion), kind=kOutput, calls=%fused_computation.4 | convolution fusion | flops 51380224 | bytes 5243904 | tf_op jit(solution)/shard_map/tsc,bsc->btc/dot_general | solution.py:62
  238.0 30.1 %while.14 = (s32[]{:T(128)}, f32[16,1024]{1,0:T(8,128)S(1)}, s32[]{:T(128)}, f32[32,16,1024]{2,1,0:T(8,128)}, f32[32,16,1024]{2,1,0:T(8,128)}, /*index=5*/s32[]{:T(128)}, s32[]{:T(128)}) while((s32[]{:T(128)}, f32[16,1024]{1,0:T(8,128)S(1)}, s32[]{:T(128)}, f32[32,16,1024]{2,1,0:T(8,128)}, f32[32,16,1024]{2,1,0:T(8,128)}, ...), condition=%wide.region_2.3_spmd.clone, body=%wide.region_1.2_spmd.clone.sunk | while | flops 65540 | bytes 262253 | solution.py:28
  238.0 1.1 fusion.45
  243.8 0.9 fusion.45
  244.7 0.9 fusion.45
  268.1 1.0 multiply_add_fusion
  269.2 1.7 copy.68
  270.9 12.9 %add_bitcast_fusion = f32[4,32,1024]{1,0,2:T(4,128)} fusion(f32[1024,4,32]{2,1,0:T(4,128)S(1)} %copy-done.2, f32[4,16,1024]{1,0,2:T(4,128)} %copy.68, f32[32]{0:T(128)S(1)} %iota_add_fusion, f32[16,1024]{0,1:T(8,128)S(1)} %copy.62, f32[16,1024]{0,1:T(8,128)S(1)} %copy-done.3), kind=kOutput, calls=%fused_computation.27 | convolution fusion | flops 26345472 | bytes 1441920 | tf_op jit(solution)/shard_map/tpc,bpc->btc/dot_general | solution.py:76
  283.8 2.0 copy.69
  (98 shorter events, 33.7 us)
Async XLA Ops:
  6.5 28.5 %all-gather.6.cloned.1.call-start = ((), (), s32[]{:S(2)}) async-start(), calls=%async_computation | async-start | bytes 1310720 | tf_op jit(solution)/shard_map/all_gather | solution.py:38
  7.3 121.9 %all-gather.8.cloned.1.call-start = ((), (), s32[]{:S(2)}) async-start(), calls=%async_computation.1 | async-start | bytes 25952256 | tf_op jit(solution)/shard_map/all_gather | solution.py:39
  8.0 230.0 %all-gather.12.cloned.1.call-start = ((), (), s32[]{:S(2)}) async-start(), calls=%async_computation.3 | async-start | bytes 2162688 | tf_op jit(solution)/shard_map/all_gather | solution.py:16
  9.5 136.3 %copy-start.11 = (f32[16,1024]{1,0:T(8,128)}, f32[16,1024]{1,0:T(8,128)S(1)}, u32[]{:S(2)}) copy-start(f32[16,1024]{1,0:T(8,128)S(1)} %get-tuple-element.144) | copy-start | bytes 196612
  9.6 228.4 %all-gather.10.cloned.1.call-start = ((), (), s32[]{:S(2)}) async-start(), calls=%async_computation.2 | async-start | bytes 2162688 | tf_op jit(solution)/shard_map/all_gather | solution.py:16
  35.1 99.1 %copy-start.15 = (bf16[128,4096]{1,0:T(8,128)(2,1)S(1)}, bf16[128,4096]{1,0:T(8,128)(2,1)}, u32[]{:S(2)}) copy-start(bf16[128,4096]{1,0:T(8,128)(2,1)} %all-gather.6.cloned.1.call-done) | copy-start | bytes 3145732
  143.5 7.2 %collective-permute-start = (bf16[3,2,1024]{2,1,0:T(2,128)(2,1)S(1)}, bf16[3,2,1024]{2,1,0:T(2,128)(2,1)S(1)}, u32[]{:S(2)}, u32[]{:S(2)}) collective-permute-start(bf16[3,2,1024]{2,1,0:T(2,128)(2,1)S(1)} %pad_maximum_fusion.1), channel_id=1, source_target_pairs={{0,4},{4,8},{8,12},{12,16},{16,20},{20,24},{24,28},{28,32},{32,36}... | collective-permute-start | bytes 36872 | tf_op jit(solution)/shard_map/ppermute | solution.py:11
  151.6 1.1 copy-start
  168.4 1.9 copy-start.6
  168.4 2.7 copy-start.13
  170.3 0.8 copy-start.4
  170.4 0.7 copy-start.7
  170.4 0.8 copy-start.9
  193.1 14.5 %copy-start.5 = (f32[1024,4,16]{0,2,1:T(8,128)S(1)}, f32[1024,4,16]{0,2,1:T(8,128)}, u32[]{:S(2)}) copy-start(f32[1024,4,16]{0,2,1:T(8,128)} %copy-done.4) | copy-start | bytes 786436
  193.1 14.5 %copy-start.8 = (f32[1,16,1024]{2,1,0:T(8,128)S(1)}, f32[1,16,1024]{2,1,0:T(8,128)}, u32[]{:S(2)}) copy-start(f32[1,16,1024]{2,1,0:T(8,128)} %copy-done.7) | copy-start | bytes 196612
  193.1 14.5 %copy-start.10 = (f32[1,16,1024]{2,1,0:T(8,128)S(1)}, f32[1,16,1024]{2,1,0:T(8,128)}, u32[]{:S(2)}) copy-start(f32[1,16,1024]{2,1,0:T(8,128)} %copy-done.9) | copy-start | bytes 196612
  208.4 59.7 %copy-start.12 = (f32[16,1024]{1,0:T(8,128)S(1)}, f32[16,1024]{1,0:T(8,128)}, u32[]{:S(2)}) copy-start(f32[16,1024]{1,0:T(8,128)} %copy-done.11) | copy-start | bytes 196612
  238.0 32.9 %copy-start.2 = (f32[1024,4,32]{2,1,0:T(4,128)S(1)}, f32[1024,4,32]{2,1,0:T(4,128)}, u32[]{:S(2)}) copy-start(f32[1024,4,32]{2,1,0:T(4,128)} %fusion.1) | copy-start | bytes 1572868
  238.0 32.9 %copy-start.3 = (f32[16,1024]{0,1:T(8,128)S(1)}, f32[16,1024]{0,1:T(8,128)}, u32[]{:S(2)}) copy-start(f32[16,1024]{0,1:T(8,128)} %copy.61) | copy-start | bytes 196612
  283.8 2.0 copy-start.1
  283.8 2.0 copy-start.14
Sparse Core Ops, SparseCore 0:
  9.0 25.9 all-gather.5
  37.4 91.7 all-gather.7
  131.4 43.6 all-gather.11
  177.3 43.2 all-gather.9
where the time goes:
time: 295 us; the launch traced here: 293 us
  waiting for transfers between devices  125 us (42%)
  matrix products  71.5 us (24%)
  other arithmetic  49.9 us (17%)
  local copies, waits for them, and re-layouts  30.4 us (10%)
  between operations  13.5 us (5%)
    all_gather x1, waiting for transfers between devices, per_device(): piece = lax.all_gather(in_weight, 'ctx', axis=0, tiled=True)  94.1 us
    dot_general x1, matrix products, per_device(): jnp.einsum('tsc,bsc->btc', toeplitz, blocked, precision=lax.Precision.HIG...  29.5 us
    select_n x32, other arithmetic, turn(): return jax.tree.map(lambda a, b: jnp.where(reached, a, b), new, before)  29.4 us
    all_gather x1, waiting for transfers between devices, per_device(): whole = lax.all_gather(tokens, 'tp', axis=1, tiled=True)  24.7 us
    gather x2, local copies, waits for them, and re-layouts, per_device(): response[jnp.clip(lags, 0, span - 1)]  19.8 us
    reduce_sum x1, other arithmetic, per_device(): response = jnp.sum(residue[None] * powers, axis=1)  15.3 us
    dot_general x1, matrix products, per_device(): jnp.einsum('spc,bsc->bpc', tails, blocked, precision=lax.Precision.HIGHEST)  14.8 us
    dot_general x3, matrix products, per_device(): jnp.dot(whole, piece[:, g, :], preferred_element_type=jnp.float32)  14.3 us
  transfers between devices with their start and end apart: 5, of which 3 were waited for; matrix products, arithmetic and copies ran while one was open for 35% of the time, Pallas kernels for 0%

commit v1 on v0

--- a/solution.py
+++ b/solution.py
@@ -3,6 +3,16 @@
 import jax.numpy as jnp
 from jax import lax
 from jax.sharding import PartitionSpec as P
+
+
+def turned_line(shard, axis, dim):
+    size = lax.axis_size(axis)
+    moving, blocks = (shard, [shard])
+    for _ in range(size - 1):
+        moving = lax.ppermute(moving, axis, [(i, (i + 1) % size) for i in range(size)])
+        blocks.insert(0, moving)
+    merged = jnp.concatenate(blocks, axis=dim)
+    return jnp.roll(merged, (lax.axis_index(axis) + 1) * shard.shape[dim], axis=dim)
 
 
 def passed_along(array, axis, by):
@@ -35,7 +45,7 @@
 def per_device(tokens, in_weight, conv_taps, decay_rate, residue, skip):
     rows = tokens.shape[0]
     chans = in_weight.shape[2]
-    whole = lax.all_gather(tokens, "tp", axis=1, tiled=True)
+    whole = turned_line(tokens, "tp", 1)
     piece = lax.all_gather(in_weight, "ctx", axis=0, tiled=True)
     sums = tuple(
         (jnp.dot(whole, piece[:, g, :], preferred_element_type=jnp.float32) for g in range(3))

time: 295 us -> 270 us (0.915)
  waiting for transfers between devices: 125 us -> 90.9 us
  local copies, waits for them, and re-layouts: 30.4 us -> 36.4 us
    all_gather x1, waiting for transfers between devices: 94.1 us -> 64.3 us  [per_device(): piece = lax.all_gather(in_weight, 'ctx', axis=0, tiled=True)]
    all_gather x1 -> x0, waiting for transfers between devices: 24.7 us -> none  [per_device(): whole = lax.all_gather(tokens, 'tp', axis=1, tiled=True)]
    ppermute x0 -> x3, waiting for transfers between devices: none -> 21.3 us  [turned_line(): lax.ppermute(moving, axis, [(i, (i + 1) % size) for i in range(size)])]
    unnamed x34 -> x41, local copies, waits for them, and re-layouts: 2.25 us -> 7.44 us
  transfers between devices with their start and end apart: 5 -> 7, of which waited for: 3 -> 5; matrix products, arithmetic and copies ran while one was open for 35% -> 41% of each run, Pallas kernels for 0% -> 0%
where the time goes in v1:
time: 270 us; the launch traced here: 268 us
  waiting for transfers between devices  90.9 us (34%)
  matrix products  72.2 us (27%)
  other arithmetic  49.9 us (18%)
  local copies, waits for them, and re-layouts  36.4 us (13%)
  between operations  13.5 us (5%)
  starting transfers between devices  4.39 us (2%)
    all_gather x1, waiting for transfers between devices, per_device(): piece = lax.all_gather(in_weight, 'ctx', axis=0, tiled=True)  64.3 us
    dot_general x1, matrix products, per_device(): jnp.einsum('tsc,bsc->btc', toeplitz, blocked, precision=lax.Precision.HIG...  29.5 us
    select_n x32, other arithmetic, turn(): return jax.tree.map(lambda a, b: jnp.where(reached, a, b), new, before)  29.4 us
    ppermute x3, waiting for transfers between devices, turned_line(): lax.ppermute(moving, axis, [(i, (i + 1) % size) for i in range(size)])  21.3 us
    gather x2, local copies, waits for them, and re-layouts, per_device(): response[jnp.clip(lags, 0, span - 1)]  19.8 us
    reduce_sum x1, other arithmetic, per_device(): response = jnp.sum(residue[None] * powers, axis=1)  15.3 us
    dot_general x3, matrix products, per_device(): jnp.dot(whole, piece[:, g, :], preferred_element_type=jnp.float32)  15 us
    dot_general x1, matrix products, per_device(): jnp.einsum('spc,bsc->bpc', tails, blocked, precision=lax.Precision.HIGHEST)  14.8 us
  transfers between devices with their start and end apart: 7, of which 5 were waited for; matrix products, arithmetic and copies ran while one was open for 41% of the time, Pallas kernels for 0%

profile of v1, /device:TPU:32, one launch (start us, length us, event | category | flops | bytes accessed | tf_op | source)
XLA Modules:
  0.0 268.0 jit_solution(16639440447974538050)
XLA Ops:
  7.3 1.6 collective-permute-start
  8.9 8.0 %collective-permute-done = bf16[128,1024]{1,0:T(8,128)(2,1)S(1)} collective-permute-done((bf16[128,1024]{1,0:T(8,128)(2,1)}, bf16[128,1024]{1,0:T(8,128)(2,1)S(1)}, u32[]{:S(2)}, u32[]{:S(2)}) %collective-permute-start) | collective-permute-done | bytes 262176 | tf_op jit(solution)/shard_map/ppermute | solution.py:12
  17.2 8.2 %collective-permute-done.1 = bf16[128,1024]{1,0:T(8,128)(2,1)S(1)} collective-permute-done((bf16[128,1024]{1,0:T(8,128)(2,1)S(1)}, bf16[128,1024]{1,0:T(8,128)(2,1)S(1)}, u32[]{:S(2)}, u32[]{:S(2)}) %collective-permute-start.1) | collective-permute-done | bytes 262176 | tf_op jit(solution)/shard_map/ppermute | solution.py:12
  25.4 1.5 multiply_exponential_fusion
  27.7 5.2 %collective-permute-done.2 = bf16[128,1024]{1,0:T(8,128)(2,1)S(1)} collective-permute-done((bf16[128,1024]{1,0:T(8,128)(2,1)S(1)}, bf16[128,1024]{1,0:T(8,128)(2,1)S(1)}, u32[]{:S(2)}, u32[]{:S(2)}) %collective-permute-start.2) | collective-permute-done | bytes 262176 | tf_op jit(solution)/shard_map/ppermute | solution.py:12
  38.9 64.3 %all-gather.5.cloned.1.call-done = bf16[4096,3,1024]{2,0,1:T(8,128)(2,1)} async-done(((bf16[128,3,1024]{2,0,1:T(8,128)(2,1)}), bf16[4096,3,1024]{2,0,1:T(8,128)(2,1)}) %all-gather.5.cloned.1.call-update) | async-done | bytes 25165840 | tf_op jit(solution)/shard_map/all_gather | solution.py:49
  103.2 5.0 %fusion.29 = bf16[1,128,1024]{2,1,0:T(8,128)(2,1)S(1)} fusion(bf16[4096,3,1024]{2,0,1:T(8,128)(2,1)} %all-gather.5.cloned.1.call-done, bf16[128,8192]{1,0:T(8,128)(2,1)} %constant_dynamic-update-slice_fusion, s32[]{:T(128)S(6)} %select_n.50), kind=kOutput, calls=%fused_computation.38 | convolution fusion | flops 1073872896 | bytes 9699332 | tf_op jit(solution)/shard_map/dot_general | solution.py:51
  108.2 5.0 %fusion.28 = bf16[1,128,1024]{2,1,0:T(8,128)(2,1)S(1)} fusion(bf16[4096,3,1024]{2,0,1:T(8,128)(2,1)} %all-gather.5.cloned.1.call-done, bf16[128,8192]{1,0:T(8,128)(2,1)} %constant_dynamic-update-slice_fusion, s32[]{:T(128)S(6)} %select_n.50), kind=kOutput, calls=%fused_computation.37 | convolution fusion | flops 1073872896 | bytes 9699332 | tf_op jit(solution)/shard_map/dot_general | solution.py:51
  113.1 5.1 %fusion.27 = bf16[1,128,1024]{2,1,0:T(8,128)(2,1)S(1)} fusion(bf16[4096,3,1024]{2,0,1:T(8,128)(2,1)} %all-gather.5.cloned.1.call-done, bf16[128,8192]{1,0:T(8,128)(2,1)} %constant_dynamic-update-slice_fusion, s32[]{:T(128)S(6)} %select_n.50), kind=kOutput, calls=%fused_computation.36 | convolution fusion | flops 1073872896 | bytes 9699332 | tf_op jit(solution)/shard_map/dot_general | solution.py:51
  118.2 2.4 collective-permute-start.3
  120.8 4.5 %collective-permute-done.3 = bf16[3,2,1024]{2,1,0:T(2,128)(2,1)S(1)} collective-permute-done((bf16[3,2,1024]{2,1,0:T(2,128)(2,1)S(1)}, bf16[3,2,1024]{2,1,0:T(2,128)(2,1)S(1)}, u32[]{:S(2)}, u32[]{:S(2)}) %collective-permute-start.3) | collective-permute-done | bytes 12320 | tf_op jit(solution)/shard_map/ppermute | solution.py:21
  126.3 1.1 copy-done
  128.2 14.8 %fusion.10 = f32[1024,4,16]{2,1,0:T(4,128)} fusion(f32[4,32,1024]{1,0,2:T(4,128)S(1)} %copy.65, f32[32]{0:T(128)S(1)} %iota_subtract_fusion, f32[16,1024]{0,1:T(8,128)S(1)} %copy.62), kind=kOutput, calls=%fused_computation.16 | convolution fusion | flops 25690112 | bytes 852096 | tf_op jit(solution)/shard_map/spc,bsc->bpc/dot_general | solution.py:74
  143.1 2.0 copy.67
  146.9 15.3 %multiply_reduce_fusion = f32[32,1024]{0,1:T(8,128)S(1)} fusion(f32[16,1024]{0,1:T(8,128)S(1)} %copy.62, f32[16,1024]{0,1:T(8,128)} %copy.61), kind=kLoop, calls=%fused_computation.20 | loop fusion | flops 1540096 | bytes 262144 | tf_op jit(solution)/shard_map/reduce_sum | solution.py:68
  162.5 5.4 %gather_fusion = f32[1024,1024]{1,0:T(8,128)} fusion(f32[32,1024]{1,0:T(8,128)S(1)} %copy.63, s32[1024]{0:T(1024)S(1)} %broadcast_clamp_fusion), kind=kCustom, calls=%fused_computation | custom fusion | bytes 8392704 | tf_op jit(solution)/shard_map/gather | solution.py:70
  167.9 14.4 %copy.64 = f32[32,32,1024]{1,0,2:T(8,128)} copy(f32[32,32,1024]{2,1,0:T(8,128)} %bitcast.76) | data formatting | bytes 8388608 | tf_op jit(solution)/shard_map/gather | solution.py:70
  183.2 29.5 %fusion.1 = f32[1024,4,32]{2,1,0:T(4,128)} fusion(f32[4,32,1024]{1,0,2:T(4,128)S(1)} %copy.65, f32[32,32,1024]{1,0,2:T(8,128)} %copy.64, pred[32,32]{1,0:T(8,128)(4,1)S(1)} %subtract_compare_fusion), kind=kOutput, calls=%fused_computation.4 | convolution fusion | flops 51380224 | bytes 5243904 | tf_op jit(solution)/shard_map/tsc,bsc->btc/dot_general | solution.py:72
  212.8 30.1 %while.14 = (s32[]{:T(128)}, f32[16,1024]{1,0:T(8,128)S(1)}, s32[]{:T(128)}, f32[32,16,1024]{2,1,0:T(8,128)}, f32[32,16,1024]{2,1,0:T(8,128)}, /*index=5*/s32[]{:T(128)}, s32[]{:T(128)}) while((s32[]{:T(128)}, f32[16,1024]{1,0:T(8,128)S(1)}, s32[]{:T(128)}, f32[32,16,1024]{2,1,0:T(8,128)}, f32[32,16,1024]{2,1,0:T(8,128)}, ...), condition=%wide.region_2.3_spmd.clone, body=%wide.region_1.2_spmd.clone.sunk | while | flops 65540 | bytes 262245 | solution.py:38
  212.8 1.1 fusion.48
  242.9 1.0 multiply_add_fusion
  244.0 1.7 copy.68
  245.7 12.9 %add_bitcast_fusion = f32[4,32,1024]{1,0,2:T(4,128)} fusion(f32[1024,4,32]{2,1,0:T(4,128)S(1)} %copy-done.2, f32[4,16,1024]{1,0,2:T(4,128)} %copy.68, f32[32]{0:T(128)S(1)} %iota_add_fusion, f32[16,1024]{0,1:T(8,128)S(1)} %copy.62, f32[16,1024]{0,1:T(8,128)S(1)} %copy-done.3), kind=kOutput, calls=%fused_computation.27 | convolution fusion | flops 26345472 | bytes 1441920 | tf_op jit(solution)/shard_map/tpc,bpc->btc/dot_general | solution.py:86
  258.6 2.0 copy.69
  (109 shorter events, 42.0 us)
Async XLA Ops:
  6.5 28.7 %copy-start.6 = (bf16[128,1024]{1,0:T(8,128)(2,1)S(1)}, bf16[128,1024]{1,0:T(8,128)(2,1)}, u32[]{:S(2)}) copy-start(bf16[128,1024]{1,0:T(8,128)(2,1)} %param.8) | copy-start | bytes 786436
  6.5 96.6 %all-gather.5.cloned.1.call-start = ((), (), s32[]{:S(2)}) async-start(), calls=%async_computation | async-start | bytes 25952256 | tf_op jit(solution)/shard_map/all_gather | solution.py:49
  7.3 205.5 %all-gather.9.cloned.1.call-start = ((), (), s32[]{:S(2)}) async-start(), calls=%async_computation.2 | async-start | bytes 2162688 | tf_op jit(solution)/shard_map/all_gather | solution.py:26
  7.3 9.6 %collective-permute-start = (bf16[128,1024]{1,0:T(8,128)(2,1)}, bf16[128,1024]{1,0:T(8,128)(2,1)S(1)}, u32[]{:S(2)}, u32[]{:S(2)}) collective-permute-start(bf16[128,1024]{1,0:T(8,128)(2,1)} %param.8), channel_id=1, source_target_pairs={{0,1},{1,2},{2,3},{3,0},{4,5},{5,6},{6,7},{7,4},{8,9},{9,10},{10,1... | collective-permute-start | bytes 786440 | tf_op jit(solution)/shard_map/ppermute | solution.py:12
  16.9 8.5 %collective-permute-start.1 = (bf16[128,1024]{1,0:T(8,128)(2,1)S(1)}, bf16[128,1024]{1,0:T(8,128)(2,1)S(1)}, u32[]{:S(2)}, u32[]{:S(2)}) collective-permute-start(bf16[128,1024]{1,0:T(8,128)(2,1)S(1)} %collective-permute-done), channel_id=1, source_target_pairs={{0,1},{1,2},{2,3},{3,0},{4,5},{5,6},{6,7},{7,4},{8,9},{9,10},{10,1... | collective-permute-start | bytes 786440 | tf_op jit(solution)/shard_map/ppermute | solution.py:12
  25.4 7.6 %collective-permute-start.2 = (bf16[128,1024]{1,0:T(8,128)(2,1)S(1)}, bf16[128,1024]{1,0:T(8,128)(2,1)S(1)}, u32[]{:S(2)}, u32[]{:S(2)}) collective-permute-start(bf16[128,1024]{1,0:T(8,128)(2,1)S(1)} %collective-permute-done.1), channel_id=1, source_target_pairs={{0,1},{1,2},{2,3},{3,0},{4,5},{5,6},{6,7},{7,4},{8,9},{9,10},{10,1... | collective-permute-start | bytes 786440 | tf_op jit(solution)/shard_map/ppermute | solution.py:12
  26.8 93.8 %copy-start.12 = (f32[16,1024]{1,0:T(8,128)}, f32[16,1024]{1,0:T(8,128)S(1)}, u32[]{:S(2)}) copy-start(f32[16,1024]{1,0:T(8,128)S(1)} %get-tuple-element.144) | copy-start | bytes 196612
  26.9 185.9 %all-gather.7.cloned.1.call-start = ((), (), s32[]{:S(2)}) async-start(), calls=%async_computation.1 | async-start | bytes 2162688 | tf_op jit(solution)/shard_map/all_gather | solution.py:26
  118.2 7.1 %collective-permute-start.3 = (bf16[3,2,1024]{2,1,0:T(2,128)(2,1)S(1)}, bf16[3,2,1024]{2,1,0:T(2,128)(2,1)S(1)}, u32[]{:S(2)}, u32[]{:S(2)}) collective-permute-start(bf16[3,2,1024]{2,1,0:T(2,128)(2,1)S(1)} %pad_maximum_fusion.1), channel_id=1, source_target_pairs={{0,4},{4,8},{8,12},{12,16},{16,20},{20,24},{24,28},{28,32},{32,36}... | collective-permute-start | bytes 36872 | tf_op jit(solution)/shard_map/ppermute | solution.py:21
  126.2 1.1 copy-start
  143.1 2.0 copy-start.7
  143.1 2.8 %copy-start.14 = (f32[16,1024]{1,0:T(8,128)S(1)}, f32[16,1024]{1,0:T(8,128)}, u32[]{:S(2)}) copy-start(f32[16,1024]{1,0:T(8,128)} %param.12) | copy-start | bytes 196612
  145.1 0.8 copy-start.4
  145.1 0.7 copy-start.8
  145.1 0.8 copy-start.10
  167.9 14.5 %copy-start.5 = (f32[1024,4,16]{0,2,1:T(8,128)S(1)}, f32[1024,4,16]{0,2,1:T(8,128)}, u32[]{:S(2)}) copy-start(f32[1024,4,16]{0,2,1:T(8,128)} %copy-done.4) | copy-start | bytes 786436
  167.9 14.5 %copy-start.9 = (f32[1,16,1024]{2,1,0:T(8,128)S(1)}, f32[1,16,1024]{2,1,0:T(8,128)}, u32[]{:S(2)}) copy-start(f32[1,16,1024]{2,1,0:T(8,128)} %copy-done.8) | copy-start | bytes 196612
  167.9 14.5 %copy-start.11 = (f32[1,16,1024]{2,1,0:T(8,128)S(1)}, f32[1,16,1024]{2,1,0:T(8,128)}, u32[]{:S(2)}) copy-start(f32[1,16,1024]{2,1,0:T(8,128)} %copy-done.10) | copy-start | bytes 196612
  183.2 59.7 %copy-start.13 = (f32[16,1024]{1,0:T(8,128)S(1)}, f32[16,1024]{1,0:T(8,128)}, u32[]{:S(2)}) copy-start(f32[16,1024]{1,0:T(8,128)} %copy-done.12) | copy-start | bytes 196612
  212.8 32.9 %copy-start.2 = (f32[1024,4,32]{2,1,0:T(4,128)S(1)}, f32[1024,4,32]{2,1,0:T(4,128)}, u32[]{:S(2)}) copy-start(f32[1024,4,32]{2,1,0:T(4,128)} %fusion.1) | copy-start | bytes 1572868
  212.8 32.9 %copy-start.3 = (f32[16,1024]{0,1:T(8,128)S(1)}, f32[16,1024]{0,1:T(8,128)}, u32[]{:S(2)}) copy-start(f32[16,1024]{0,1:T(8,128)} %copy.61) | copy-start | bytes 196612
  258.6 2.0 copy-start.1
  258.6 2.0 copy-start.15
Sparse Core Ops, SparseCore 0:
  9.7 93.4 all-gather.4
  105.4 43.7 all-gather.8
  151.5 43.2 all-gather.6
